TPU v7x, 32 devices: a whole 2x2x4 slice. The times are simulated.
32 devices in a mesh: sec: 4 (over x, core), key: 8 (over z, y).
Axes of the slice: x: 2, y: 2, z: 4, core: 2. Of those that a mesh axis runs over, the one named last changes fastest.
Arguments:
- query: bfloat16 [4096, 16, 128], P(('sec', 'key')), may hold values from -64 to 64
- key: bfloat16 [4096, 4, 128], P(('sec', 'key')), may hold values from -5 to 5
- value: bfloat16 [4096, 4, 128], P(('sec', 'key')), may hold values from -5 to 5
- raw_directions: bfloat16 [4096, 4, 128], P(('sec', 'key')), may hold values from -5 to 5
- beta_raw_logits: float32 [4096, 4], P(('sec', 'key')), may hold values from -7 to 7
Outputs:
- attended: bfloat16 [4096, 16, 128], P(('sec', 'key'))
All inputs are finite; a program needn't handle non-finite values.
Results may differ from a plain program's by a relative error of at most 0.0055.
Values sent between devices are 32-bit elements; how exact they have to be, the bound alone decides.
No kernel may reach another device: no remote copies, remote signals or barrier semaphores. Data moves between devices by JAX's collectives and lax.ppermute only.
A program may use at most 64 MiB of HBM per device.

v0:
```python
import math
import jax
import jax.numpy as jnp
from jax import lax
from jax.sharding import PartitionSpec as P

highest = lax.Precision.HIGHEST


def carried_in(value, axis, join, neutral, backward):
    count, mine = (lax.axis_size(axis), lax.axis_index(axis))
    pieces = lax.all_gather(value, axis)
    if backward:
        pieces = pieces[::-1]
        mine = count - 1 - mine
    total = jnp.full_like(value, 0) + jnp.asarray(neutral, value.dtype)

    def turn(position, total):
        longer = join(total, pieces[position])
        return jnp.where(position < mine, longer, total)

    return lax.fori_loop(0, count - 1, turn, total)


def shifted(value, axis, steps):
    count = lax.axis_size(axis)
    first, last = (max(0, -steps), min(count, count - steps))
    return lax.ppermute(value, axis, [(source, source + steps) for source in range(first, last)])


def block_terms(query, key, raw_directions, beta_raw_logits):
    length = key.shape[0]
    heads = key.shape[1]
    width = key.shape[2]
    query_group = query.shape[1] // heads
    w_float = raw_directions.astype(jnp.float32)
    w_unit = w_float / jnp.sqrt(jnp.sum(w_float * w_float, -1, keepdims=True) + 1e-06)
    beta = 2.0 * jax.nn.sigmoid(beta_raw_logits)
    w_heads = jnp.transpose(w_unit, (1, 0, 2))
    k_heads = jnp.transpose(key.astype(jnp.float32), (1, 0, 2))
    b_heads = jnp.transpose(beta, (1, 0))[:, :, None]
    positions = jnp.arange(length)
    strict = (positions[:, None] > positions[None, :]).astype(jnp.float32)
    lower = (positions[:, None] >= positions[None, :]).astype(jnp.float32)
    gram = jnp.einsum("hte,hse->hts", w_heads, w_heads, precision=highest) * strict
    system = jnp.eye(length, dtype=jnp.float32) + b_heads * gram
    cross = jnp.einsum("hte,hse->hts", w_heads, k_heads, precision=highest) * strict
    right = jnp.concatenate([b_heads * w_heads, b_heads * cross], axis=2)
    solved = lax.linalg.triangular_solve(
        system, right, left_side=True, lower=True, unit_diagonal=True
    )
    y_rows = solved[:, :, :width]
    z_rows = solved[:, :, width:]
    block_map = jnp.eye(width, dtype=jnp.float32) - jnp.einsum(
        "hte,htf->hef", w_heads, y_rows, precision=highest
    )
    key_end = k_heads - jnp.einsum("hts,hte->hse", z_rows, w_heads, precision=highest)
    q_heads = jnp.transpose(
        query.astype(jnp.float32).reshape(length, heads, query_group, width), (1, 2, 0, 3)
    )
    q_dot_w = jnp.einsum("hgie,hte->hgit", q_heads, w_heads, precision=highest) * lower
    query_start = q_heads - jnp.einsum("hgit,hte->hgie", q_dot_w, y_rows, precision=highest)
    inner = jnp.einsum("hgie,hje->hgij", q_heads, k_heads, precision=highest)
    inner = inner - jnp.einsum("hgit,htj->hgij", q_dot_w, z_rows, precision=highest)
    query_start = query_start.reshape(heads, query_group * length, width)
    inner = inner.reshape(heads, query_group * length, length) * width ** (-0.5)
    return (query_start, key_end, block_map, inner)


def attend(state, scores, values, valid):
    score_maxima, weighted_totals, exponent_sums = state
    masked = jnp.where(valid, scores, -1e30)
    new_max = jnp.maximum(score_maxima, jnp.max(masked, -1))
    weights = jnp.where(valid, jnp.exp(masked - new_max[..., None]), 0.0)
    factor = jnp.exp(score_maxima - new_max)
    weighted_totals = weighted_totals * factor + jnp.sum(weights, -1)
    rounded = weights.astype(jnp.bfloat16)
    exponent_sums = exponent_sums * factor[..., None] + jnp.einsum(
        "...ij,...je->...ie", rounded, values, preferred_element_type=jnp.float32
    )
    return (new_max, weighted_totals, exponent_sums)


def attend_packet(state, queries_flat, packet, valid, width):
    count = packet.shape[0]
    block = math.gcd(count, 512)
    scale_factor = width ** (-0.5)

    def one_block(index, carry):
        piece = lax.dynamic_slice_in_dim(packet, index * block, block, 0)
        scores = (
            jnp.einsum("ie,je->ij", queries_flat, piece[:, :width], precision=highest)
            * scale_factor
        )
        return attend(carry, scores, piece[:, width:].astype(jnp.bfloat16), valid)

    return lax.fori_loop(0, count // block, one_block, state)


def later_first(earlier, later):
    return jnp.einsum("hij,hjk->hik", later, earlier, precision=highest)


def earlier_first(earlier, later):
    return jnp.einsum("hij,hjk->hik", earlier, later, precision=highest)


def body(query, key, value, raw_directions, beta_raw_logits):
    length = query.shape[0]
    q_count = query.shape[1]
    width = query.shape[2]
    kv_heads = key.shape[1]
    query_group = q_count // kv_heads
    key_count = lax.axis_size("key")
    sec_count = lax.axis_size("sec")
    key_index = lax.axis_index("key")
    sec_index = lax.axis_index("sec")
    per_slot = q_count // key_count
    repeat_count = key_count // kv_heads
    rows_section = length * key_count
    scale_factor = width ** (-0.5)
    query_start, key_end, block_map, inner = block_terms(
        query, key, raw_directions, beta_raw_logits
    )
    value_head_rows = jnp.transpose(value, (1, 0, 2))
    positions = jnp.arange(length)
    causal = jnp.tile(positions[:, None] >= positions[None, :], (query_group, 1))
    local = (
        jnp.full((kv_heads, query_group * length), -1e30, jnp.float32),
        jnp.zeros((kv_heads, query_group * length), jnp.float32),
        jnp.zeros((kv_heads, query_group * length, width), jnp.float32),
    )
    local = attend(local, inner, value_head_rows, causal)
    packed = jnp.concatenate([key_end, value_head_rows.astype(jnp.float32)], axis=2)
    gathered_pack, gathered_maps = (
        lax.all_gather(packed, "key", axis=1, tiled=True),
        lax.all_gather(block_map, "key", axis=0, tiled=True),
    )
    gathered_maps = gathered_maps.reshape(key_count, kv_heads, width, width)

    def replay_step(step, carry):
        moving = carry[0]
        source = jnp.maximum(key_index - step, 0)
        piece = lax.dynamic_slice_in_dim(gathered_pack, source * length, length, 1)
        scores = (
            jnp.einsum("hie,hje->hij", moving, piece[:, :, :width], precision=highest)
            * scale_factor
        )
        state = attend(
            carry[1:], scores, piece[:, :, width:].astype(jnp.bfloat16), key_index - step >= 0
        )
        source_map = lax.dynamic_index_in_dim(gathered_maps, source, 0, keepdims=False)
        moving = jnp.einsum("hie,hef->hif", moving, source_map, precision=highest)
        return (moving,) + state

    local = lax.fori_loop(1, key_count, replay_step, (query_start,) + local)[1:]
    eye_maps = jnp.broadcast_to(jnp.eye(width, dtype=jnp.float32), block_map.shape)
    before = carried_in(block_map, "key", later_first, eye_maps, False)
    after = carried_in(block_map, "key", earlier_first, eye_maps, True)
    section_map = jnp.einsum(
        "hij,hjk->hik",
        after,
        jnp.einsum("hij,hjk->hik", block_map, before, precision=highest),
        precision=highest,
    )
    query_section = jnp.einsum("hie,hef->hif", query_start, before, precision=highest)
    query_section = jnp.transpose(
        query_section.reshape(kv_heads, query_group, length, width), (2, 0, 1, 3)
    )
    key_section = jnp.einsum("hje,hfe->hjf", key_end, after, precision=highest)
    key_pack = jnp.concatenate(
        [jnp.transpose(key_section, (1, 0, 2)), value.astype(jnp.float32)], axis=2
    )
    own_map = lax.dynamic_index_in_dim(section_map, key_index // repeat_count, 0, keepdims=False)
    query_slots = query_section.reshape(length, key_count, per_slot, width)
    key_slots = jnp.repeat(key_pack, repeat_count, axis=1)
    slot_queries, slot_keys = (
        lax.all_to_all(query_slots, "key", split_axis=1, concat_axis=0, tiled=True),
        lax.all_to_all(key_slots, "key", split_axis=1, concat_axis=0, tiled=True),
    )
    slot_flat = jnp.transpose(
        slot_queries.reshape(rows_section, per_slot, width), (1, 0, 2)
    ).reshape(per_slot * rows_section, width)
    slot_keys = slot_keys.reshape(rows_section, 2 * width)
    flat_rows = slot_flat.shape[0]
    distant = (
        jnp.full((flat_rows,), -1e30, jnp.float32),
        jnp.zeros((flat_rows,), jnp.float32),
        jnp.zeros((flat_rows, width), jnp.float32),
    )

    def walk_step(step, carry):
        arrived = shifted(carry[0], "sec", 1)
        state = attend_packet(carry[1:], slot_flat, arrived, sec_index - step >= 0, width)
        moved = jnp.einsum("je,fe->jf", arrived[:, :width], own_map, precision=highest)
        return (jnp.concatenate([moved, arrived[:, width:]], axis=1),) + state

    distant = lax.fori_loop(1, sec_count, walk_step, (slot_keys,) + distant)[1:]
    far_max = jnp.transpose(distant[0].reshape(per_slot, rows_section), (1, 0))
    far_total = jnp.transpose(distant[1].reshape(per_slot, rows_section), (1, 0))
    far_sums = jnp.transpose(distant[2].reshape(per_slot, rows_section, width), (1, 0, 2))
    back_sums, back_max, back_total = (
        lax.all_to_all(far_sums, "key", split_axis=0, concat_axis=1, tiled=True),
        lax.all_to_all(far_max, "key", split_axis=0, concat_axis=1, tiled=True),
        lax.all_to_all(far_total, "key", split_axis=0, concat_axis=1, tiled=True),
    )
    near_max = jnp.transpose(local[0].reshape(kv_heads, query_group, length), (2, 0, 1)).reshape(
        length, q_count
    )
    near_total = jnp.transpose(local[1].reshape(kv_heads, query_group, length), (2, 0, 1)).reshape(
        length, q_count
    )
    near_sums = jnp.transpose(
        local[2].reshape(kv_heads, query_group, length, width), (2, 0, 1, 3)
    ).reshape(length, q_count, width)
    joint_max = jnp.maximum(near_max, back_max)
    near_factor = jnp.exp(near_max - joint_max)
    far_factor = jnp.exp(back_max - joint_max)
    weighted_totals = near_total * near_factor + back_total * far_factor
    exponent_sums = near_sums * near_factor[..., None] + back_sums * far_factor[..., None]
    return (exponent_sums / weighted_totals[..., None]).astype(jnp.bfloat16)


def solution(mesh):
    return jax.shard_map(
        body,
        mesh=mesh,
        in_specs=(
            P(("sec", "key"), None, None),
            P(("sec", "key"), None, None),
            P(("sec", "key"), None, None),
            P(("sec", "key"), None, None),
            P(("sec", "key"), None),
        ),
        out_specs=P(("sec", "key"), None, None),
        check_vma=False,
    )
```

profile of v0, /device:TPU:6, one launch (start us, length us, event | category | flops | bytes accessed | tf_op | source)
XLA Modules:
  0.0 414.8 jit_solution(6768845351763684802)
XLA Ops:
  11.4 39.3 %custom-call.3 = f32[4,1,128,128]{2,3,1,0:T(8,128)S(1)} custom-call(f32[4,1,128,128]{3,2,1,0:T(8,128)S(1)} %fusion.41), custom_call_target="InvertDiagBlocksLowerTriangular" | custom-call | tf_op jit(solution)/shard_map/triangular_solve | solution.py:49
  60.5 44.1 %all-gather.4.cloned.1.call-done = f32[32,128,128]{2,1,0:T(8,128)} async-done(((f32[4,128,128]{2,1,0:T(8,128)}), f32[32,128,128]{2,1,0:T(8,128)}) %all-gather.4.cloned.1.call-update) | async-done | bytes 2097168 | tf_op jit(solution)/shard_map/all_gather | solution.py:137
  104.6 3.2 rev.3
  107.8 9.8 %while.97 = (s32[]{:T(128)}, f32[4,128,128]{2,1,0:T(8,128)S(1)}, s32[]{:T(128)}, f32[8,4,128,128]{3,2,1,0:T(8,128)}, s32[]{:T(128)}) while((s32[]{:T(128)}, f32[4,128,128]{2,1,0:T(8,128)S(1)}, s32[]{:T(128)}, f32[8,4,128,128]{3,2,1,0:T(8,128)}, s32[]{:T(128)}) %tuple.182), condition=%wide.region_10.11_spmd, body=%wide.region_9.10_spmd.sunk | while | flops 100728832 | bytes 1573447 | solution.py:22
  117.6 2.0 fusion.84
  119.6 4.9 %all-to-all-start.1 = ((f32[128,8,2,128]{3,0,2,1:T(8,128)}), f32[128,8,2,128]{3,0,2,1:T(8,128)S(1)}, u32[]{:S(2)}, u32[]{:S(2)}) async-start(f32[128,8,2,128]{3,0,2,1:T(8,128)} %bitcast.46), calls=%async_computation.1 | async-start | bytes 2097152 | tf_op jit(solution)/shard_map/all_to_all | solution.py:178
  124.6 11.2 %while.96 = (s32[]{:T(128)}, f32[4,128,128]{1,2,0:T(8,128)S(1)}, s32[]{:T(128)}, f32[8,4,128,128]{3,2,1,0:T(8,128)}, s32[]{:T(128)}) while((s32[]{:T(128)}, f32[4,128,128]{1,2,0:T(8,128)S(1)}, s32[]{:T(128)}, f32[8,4,128,128]{3,2,1,0:T(8,128)}, s32[]{:T(128)}) %tuple.165), condition=%wide.region_8.9_spmd, body=%wide.region_7.8_spmd.sunk | while | flops 100728832 | bytes 1573447 | solution.py:22
  136.5 12.3 %all-to-all-done.1 = f32[128,8,2,128]{3,0,2,1:T(8,128)S(1)} async-done(((f32[128,8,2,128]{3,0,2,1:T(8,128)}), f32[128,8,2,128]{3,0,2,1:T(8,128)S(1)}, u32[]{:S(2)}, u32[]{:S(2)}) %all-to-all-start.1) | async-done | bytes 1048608 | tf_op jit(solution)/shard_map/all_to_all | solution.py:178
  149.9 4.3 %all-to-all-start = ((f32[128,8,256]{0,2,1:T(8,128)}), f32[128,8,256]{0,2,1:T(8,128)S(1)}, u32[]{:S(2)}, u32[]{:S(2)}) async-start(f32[128,8,256]{0,2,1:T(8,128)} %bitcast.228), calls=%async_computation | async-start | bytes 2097152 | tf_op jit(solution)/shard_map/all_to_all | solution.py:179
  157.3 36.5 %all-to-all-done = f32[128,8,256]{0,2,1:T(8,128)S(1)} async-done(((f32[128,8,256]{0,2,1:T(8,128)}), f32[128,8,256]{0,2,1:T(8,128)S(1)}, u32[]{:S(2)}, u32[]{:S(2)}) %all-to-all-start) | async-done | bytes 1048608 | tf_op jit(solution)/shard_map/all_to_all | solution.py:179
  195.5 122.5 %while.99 = (s32[]{:T(128)}, f32[1024,256]{0,1:T(8,128)S(1)}, f32[2048]{0:T(1024)S(1)}, f32[2048]{0:T(1024)S(1)}, f32[2048,128]{1,0:T(8,128)}, /*index=5*/f32[12...) while((s32[]{:T(128)}, f32[1024,256]{0,1:T(8,128)S(1)}, ...), condition=%wide.region_16.17_spmd, body=%wide.region_11.16_spmd.sunk | while | flops 2094796800 | bytes 44106204 | solution.py:198
  197.4 14.2 %collective-permute-done = f32[1024,256]{0,1:T(8,128)S(1)} collective-permute-done((f32[1024,256]{0,1:T(8,128)S(1)}, f32[1024,256]{0,1:T(8,128)S(1)}, u32[]{:S(2)}, u32[]{:S(2)}) %collective-permute-start) | collective-permute-done | bytes 1048608 | tf_op jit(solution)/shard_map/while/body/eval_jaxpr/ppermute | solution.py:28
  211.6 24.0 %while.100 = (s32[]{:T(128)}, f32[2048]{0:T(1024)S(1)}, f32[2048]{0:T(1024)S(1)}, f32[2048,128]{1,0:T(8,128)}, pred[]{:T(512)}, /*index=5*/f32[1024,256]{0,1:T(8...) while((s32[]{:T(128)}, f32[2048]{0:T(1024)S(1)}, ...), condition=%wide.region_15.15_spmd, body=%wide.region_12.14_spmd.sunk | while | flops 1893208064 | bytes 35651772 | solution.py:97
  211.8 3.8 fusion.150
  215.6 2.0 copy-done
  218.8 4.9 %convolution_add_fusion.6 = f32[2048,128]{1,0:T(8,128)} fusion(f32[512,2048]{1,0:T(8,128)} %copy-done, f32[2048]{0:T(1024)S(1)} %max.48, pred[]{:T(512)} %get-tuple-element.1047, f32[2048,128]{1,0:T(8,128)} %get-tuple-element.1035, f32[2048]{0:T(1024)S(1)} %get-tuple-element.1020, bf16[512,128]{1,0:T(8,128)(2,1)S(1)} %copy.255), kind=kOutput, calls=%fused_computation.33.clone.1 | convolution fusion | flops 274202624 | bytes 6438913 | tf_op jit(solution)/shard_map/while/body/eval_jaxpr/while/body/eval_jaxpr/...ij,...je->...ie/dot_general | solution.py:78
  223.9 3.8 fusion.150
  227.7 2.0 copy-done
  230.8 4.9 %convolution_add_fusion.6 = f32[2048,128]{1,0:T(8,128)} fusion(f32[512,2048]{1,0:T(8,128)} %copy-done, f32[2048]{0:T(1024)S(1)} %max.48, pred[]{:T(512)} %get-tuple-element.1047, f32[2048,128]{1,0:T(8,128)} %get-tuple-element.1035, f32[2048]{0:T(1024)S(1)} %get-tuple-element.1020, bf16[512,128]{1,0:T(8,128)(2,1)S(1)} %copy.255), kind=kOutput, calls=%fused_computation.33.clone.1 | convolution fusion | flops 274202624 | bytes 6438913 | tf_op jit(solution)/shard_map/while/body/eval_jaxpr/while/body/eval_jaxpr/...ij,...je->...ie/dot_general | solution.py:78
  238.3 14.2 %collective-permute-done = f32[1024,256]{0,1:T(8,128)S(1)} collective-permute-done((f32[1024,256]{0,1:T(8,128)S(1)}, f32[1024,256]{0,1:T(8,128)S(1)}, u32[]{:S(2)}, u32[]{:S(2)}) %collective-permute-start) | collective-permute-done | bytes 1048608 | tf_op jit(solution)/shard_map/while/body/eval_jaxpr/ppermute | solution.py:28
  252.5 24.0 %while.100 = (s32[]{:T(128)}, f32[2048]{0:T(1024)S(1)}, f32[2048]{0:T(1024)S(1)}, f32[2048,128]{1,0:T(8,128)}, pred[]{:T(512)}, /*index=5*/f32[1024,256]{0,1:T(8...) while((s32[]{:T(128)}, f32[2048]{0:T(1024)S(1)}, ...), condition=%wide.region_15.15_spmd, body=%wide.region_12.14_spmd.sunk | while | flops 1893208064 | bytes 35651772 | solution.py:97
  252.7 3.8 fusion.150
  256.5 2.0 copy-done
  259.7 4.8 %convolution_add_fusion.6 = f32[2048,128]{1,0:T(8,128)} fusion(f32[512,2048]{1,0:T(8,128)} %copy-done, f32[2048]{0:T(1024)S(1)} %max.48, pred[]{:T(512)} %get-tuple-element.1047, f32[2048,128]{1,0:T(8,128)} %get-tuple-element.1035, f32[2048]{0:T(1024)S(1)} %get-tuple-element.1020, bf16[512,128]{1,0:T(8,128)(2,1)S(1)} %copy.255), kind=kOutput, calls=%fused_computation.33.clone.1 | convolution fusion | flops 274202624 | bytes 6438913 | tf_op jit(solution)/shard_map/while/body/eval_jaxpr/while/body/eval_jaxpr/...ij,...je->...ie/dot_general | solution.py:78
  264.7 3.8 fusion.150
  268.5 2.0 copy-done
  271.6 4.8 %convolution_add_fusion.6 = f32[2048,128]{1,0:T(8,128)} fusion(f32[512,2048]{1,0:T(8,128)} %copy-done, f32[2048]{0:T(1024)S(1)} %max.48, pred[]{:T(512)} %get-tuple-element.1047, f32[2048,128]{1,0:T(8,128)} %get-tuple-element.1035, f32[2048]{0:T(1024)S(1)} %get-tuple-element.1020, bf16[512,128]{1,0:T(8,128)(2,1)S(1)} %copy.255), kind=kOutput, calls=%fused_computation.33.clone.1 | convolution fusion | flops 274202624 | bytes 6438913 | tf_op jit(solution)/shard_map/while/body/eval_jaxpr/while/body/eval_jaxpr/...ij,...je->...ie/dot_general | solution.py:78
  279.2 14.2 %collective-permute-done = f32[1024,256]{0,1:T(8,128)S(1)} collective-permute-done((f32[1024,256]{0,1:T(8,128)S(1)}, f32[1024,256]{0,1:T(8,128)S(1)}, u32[]{:S(2)}, u32[]{:S(2)}) %collective-permute-start) | collective-permute-done | bytes 1048608 | tf_op jit(solution)/shard_map/while/body/eval_jaxpr/ppermute | solution.py:28
  293.3 24.0 %while.100 = (s32[]{:T(128)}, f32[2048]{0:T(1024)S(1)}, f32[2048]{0:T(1024)S(1)}, f32[2048,128]{1,0:T(8,128)}, pred[]{:T(512)}, /*index=5*/f32[1024,256]{0,1:T(8...) while((s32[]{:T(128)}, f32[2048]{0:T(1024)S(1)}, ...), condition=%wide.region_15.15_spmd, body=%wide.region_12.14_spmd.sunk | while | flops 1893208064 | bytes 35651772 | solution.py:97
  293.5 3.8 fusion.150
  297.3 2.0 copy-done
  300.5 4.8 %convolution_add_fusion.6 = f32[2048,128]{1,0:T(8,128)} fusion(f32[512,2048]{1,0:T(8,128)} %copy-done, f32[2048]{0:T(1024)S(1)} %max.48, pred[]{:T(512)} %get-tuple-element.1047, f32[2048,128]{1,0:T(8,128)} %get-tuple-element.1035, f32[2048]{0:T(1024)S(1)} %get-tuple-element.1020, bf16[512,128]{1,0:T(8,128)(2,1)S(1)} %copy.255), kind=kOutput, calls=%fused_computation.33.clone.1 | convolution fusion | flops 274202624 | bytes 6438913 | tf_op jit(solution)/shard_map/while/body/eval_jaxpr/while/body/eval_jaxpr/...ij,...je->...ie/dot_general | solution.py:78
  305.5 3.8 fusion.150
  309.3 2.0 copy-done
  312.5 4.8 %convolution_add_fusion.6 = f32[2048,128]{1,0:T(8,128)} fusion(f32[512,2048]{1,0:T(8,128)} %copy-done, f32[2048]{0:T(1024)S(1)} %max.48, pred[]{:T(512)} %get-tuple-element.1047, f32[2048,128]{1,0:T(8,128)} %get-tuple-element.1035, f32[2048]{0:T(1024)S(1)} %get-tuple-element.1020, bf16[512,128]{1,0:T(8,128)(2,1)S(1)} %copy.255), kind=kOutput, calls=%fused_computation.33.clone.1 | convolution fusion | flops 274202624 | bytes 6438913 | tf_op jit(solution)/shard_map/while/body/eval_jaxpr/while/body/eval_jaxpr/...ij,...je->...ie/dot_general | solution.py:78
  318.7 3.8 all-to-all-start.2
  324.1 3.0 copy.176
  327.6 5.6 %all-to-all-start.3 = ((f32[1024,2,128]{2,1,0:T(2,128)}), f32[1024,2,128]{2,1,0:T(2,128)}, u32[]{:S(2)}, u32[]{:S(2)}) async-start(f32[1024,2,128]{2,1,0:T(2,128)} %copy.176), calls=%async_computation.3 | async-start | bytes 2097152 | tf_op jit(solution)/shard_map/all_to_all | solution.py:203
  337.8 11.0 %all-to-all-done.3 = f32[1024,2,128]{2,1,0:T(2,128)} async-done(((f32[1024,2,128]{2,1,0:T(2,128)}), f32[1024,2,128]{2,1,0:T(2,128)}, u32[]{:S(2)}, u32[]{:S(2)}) %all-to-all-start.3) | async-done | bytes 1048608 | tf_op jit(solution)/shard_map/all_to_all | solution.py:203
  348.8 4.2 %all-to-all-start.4 = ((f32[8,128,2]{1,2,0:T(2,128)}), f32[8,128,2]{1,2,0:T(2,128)S(1)}, u32[]{:S(2)}, u32[]{:S(2)}) async-start(f32[8,128,2]{1,2,0:T(2,128)} %bitcast.65), calls=%async_computation.4 | async-start | bytes 16384 | tf_op jit(solution)/shard_map/all_to_all | solution.py:205
  353.0 51.2 %while.95 = (s32[]{:T(128)}, f32[4,512,128]{1,2,0:T(8,128)S(1)}, f32[4,512]{1,0:T(4,128)S(1)}, f32[4,512]{1,0:T(4,128)S(1)}, f32[4,512,128]{2,1,0:T(8,128)S(1)},...) while((s32[]{:T(128)}, f32[4,512,128]{1,2,0:T(8,128)S(1)}, ...), condition=%wide.region_6.7_spmd, body=%wide.region_3.6_spmd.sunk | while | flops 875302912 | bytes 15991019 | solution.py:156
  358.3 2.0 convolution_bitcast_fusion.5
  365.6 2.0 convolution_bitcast_fusion.5
  372.9 2.0 convolution_bitcast_fusion.5
  380.2 2.0 convolution_bitcast_fusion.5
  387.6 2.0 convolution_bitcast_fusion.5
  394.9 2.0 convolution_bitcast_fusion.5
  402.2 2.0 convolution_bitcast_fusion.5
  (290 shorter events, 104.1 us)
Async XLA Ops:
  6.5 47.1 %copy-start.9 = (bf16[128,4,128]{2,1,0:T(4,128)(2,1)S(1)}, bf16[128,4,128]{2,1,0:T(4,128)(2,1)}, u32[]{:S(2)}) copy-start(bf16[128,4,128]{2,1,0:T(4,128)(2,1)} %param.18) | copy-start | bytes 393220
  6.5 48.6 %copy-start.14 = (bf16[128,16,128]{2,1,0:T(8,128)(2,1)S(1)}, bf16[128,16,128]{2,1,0:T(8,128)(2,1)}, u32[]{:S(2)}) copy-start(bf16[128,16,128]{2,1,0:T(8,128)(2,1)} %param.15) | copy-start | bytes 1572868
  6.5 48.8 %copy-start.16 = (bf16[128,4,128]{2,1,0:T(4,128)(2,1)S(1)}, bf16[128,4,128]{2,1,0:T(4,128)(2,1)}, u32[]{:S(2)}) copy-start(bf16[128,4,128]{2,1,0:T(4,128)(2,1)} %param.17) | copy-start | bytes 393220
  6.5 98.0 %all-gather.4.cloned.1.call-start = ((), (), s32[]{:S(2)}) async-start(), calls=%async_computation.5 | async-start | bytes 2359296 | tf_op jit(solution)/shard_map/all_gather | solution.py:137
  53.6 6.8 %copy-start.7 = (f32[4,128,256]{2,1,0:T(8,128)}, f32[4,128,256]{2,1,0:T(8,128)S(1)}, u32[]{:S(2)}) copy-start(f32[4,128,256]{2,1,0:T(8,128)S(1)} %fusion.49) | copy-start | bytes 1572868
  55.3 52.4 %copy-start.5 = (bf16[128,16,128]{2,0,1:T(8,128)(2,1)}, bf16[128,16,128]{2,0,1:T(8,128)(2,1)S(1)}, u32[]{:S(2)}) copy-start(bf16[128,16,128]{2,0,1:T(8,128)(2,1)S(1)} %copy.148) | copy-start | bytes 1572868
  55.5 49.1 %copy-start.10 = (bf16[128,4,128]{0,2,1:T(8,128)(2,1)}, bf16[128,4,128]{0,2,1:T(8,128)(2,1)S(1)}, u32[]{:S(2)}) copy-start(bf16[128,4,128]{0,2,1:T(8,128)(2,1)S(1)} %copy.204) | copy-start | bytes 393220
  57.0 78.9 %copy-start.13 = (f32[4,128,128]{1,2,0:T(8,128)}, f32[4,128,128]{1,2,0:T(8,128)S(1)}, u32[]{:S(2)}) copy-start(f32[4,128,128]{1,2,0:T(8,128)S(1)} %convolution_subtract_fusion.2) | copy-start | bytes 786436
  57.6 1.0 copy-start.2
  60.4 57.2 %copy-start.4 = (f32[4,4,128,128]{3,2,1,0:T(8,128)}, f32[4,4,128,128]{3,2,1,0:T(8,128)S(1)}, u32[]{:S(2)}) copy-start(f32[4,4,128,128]{3,2,1,0:T(8,128)S(1)} %convolution_subtract_fusion.1) | copy-start | bytes 3145732
  119.6 29.2 %all-to-all-start.1 = ((f32[128,8,2,128]{3,0,2,1:T(8,128)}), f32[128,8,2,128]{3,0,2,1:T(8,128)S(1)}, u32[]{:S(2)}, u32[]{:S(2)}) async-start(f32[128,8,2,128]{3,0,2,1:T(8,128)} %bitcast.46), calls=%async_computation.1 | async-start | bytes 2097152 | tf_op jit(solution)/shard_map/all_to_all | solution.py:178
  135.8 20.3 %copy-start.12 = (f32[4,128,128]{2,1,0:T(8,128)S(1)}, f32[4,128,128]{2,1,0:T(8,128)}, u32[]{:S(2)}) copy-start(f32[4,128,128]{2,1,0:T(8,128)} %convolution_subtract_fusion.3) | copy-start | bytes 786436
  149.9 43.8 %all-to-all-start = ((f32[128,8,256]{0,2,1:T(8,128)}), f32[128,8,256]{0,2,1:T(8,128)S(1)}, u32[]{:S(2)}, u32[]{:S(2)}) async-start(f32[128,8,256]{0,2,1:T(8,128)} %bitcast.228), calls=%async_computation | async-start | bytes 2097152 | tf_op jit(solution)/shard_map/all_to_all | solution.py:179
  154.2 198.8 %all-gather.6.cloned.1.call-start = ((), (), s32[]{:S(2)}) async-start(), calls=%async_computation.6 | async-start | bytes 4718592 | tf_op jit(solution)/shard_map/all_gather | solution.py:136
  195.5 16.1 %collective-permute-start = (f32[1024,256]{0,1:T(8,128)S(1)}, f32[1024,256]{0,1:T(8,128)S(1)}, u32[]{:S(2)}, u32[]{:S(2)}) collective-permute-start(f32[1024,256]{0,1:T(8,128)S(1)} %get-tuple-element.1099), channel_id=1, source_target_pairs={{0,8},{8,16},{16,24},{1,9},{9,17},{17,25},{2,10},{10,18},{18,26},{... | collective-permute-start | bytes 3145736 | tf_op jit(solution)/shard_map/while/body/eval_jaxpr/ppermute | solution.py:28
  215.6 2.0 copy-start
  227.6 2.0 copy-start
  236.4 16.1 %collective-permute-start = (f32[1024,256]{0,1:T(8,128)S(1)}, f32[1024,256]{0,1:T(8,128)S(1)}, u32[]{:S(2)}, u32[]{:S(2)}) collective-permute-start(f32[1024,256]{0,1:T(8,128)S(1)} %get-tuple-element.1099), channel_id=1, source_target_pairs={{0,8},{8,16},{16,24},{1,9},{9,17},{17,25},{2,10},{10,18},{18,26},{... | collective-permute-start | bytes 3145736 | tf_op jit(solution)/shard_map/while/body/eval_jaxpr/ppermute | solution.py:28
  256.5 2.0 copy-start
  268.5 2.0 copy-start
  277.2 16.1 %collective-permute-start = (f32[1024,256]{0,1:T(8,128)S(1)}, f32[1024,256]{0,1:T(8,128)S(1)}, u32[]{:S(2)}, u32[]{:S(2)}) collective-permute-start(f32[1024,256]{0,1:T(8,128)S(1)} %get-tuple-element.1099), channel_id=1, source_target_pairs={{0,8},{8,16},{16,24},{1,9},{9,17},{17,25},{2,10},{10,18},{18,26},{... | collective-permute-start | bytes 3145736 | tf_op jit(solution)/shard_map/while/body/eval_jaxpr/ppermute | solution.py:28
  297.3 2.0 copy-start
  309.3 2.0 copy-start
  318.0 15.4 %copy-start.3 = (f32[4,4,128,128]{2,3,1,0:T(8,128)S(1)}, f32[4,4,128,128]{2,3,1,0:T(8,128)}, u32[]{:S(2)}) copy-start(f32[4,4,128,128]{2,3,1,0:T(8,128)} %copy-done.2) | copy-start | bytes 3145732
  318.0 15.4 %copy-start.8 = (f32[4,128,256]{2,1,0:T(8,128)S(1)}, f32[4,128,256]{2,1,0:T(8,128)}, u32[]{:S(2)}) copy-start(f32[4,128,256]{2,1,0:T(8,128)} %copy-done.7) | copy-start | bytes 1572868
  318.7 9.0 %all-to-all-start.2 = ((f32[8,128,2]{1,2,0:T(2,128)}), f32[8,128,2]{1,2,0:T(2,128)S(1)}, u32[]{:S(2)}, u32[]{:S(2)}) async-start(f32[8,128,2]{1,2,0:T(2,128)} %bitcast.53), calls=%async_computation.2 | async-start | bytes 16384 | tf_op jit(solution)/shard_map/all_to_all | solution.py:204
  322.5 12.7 %copy-start.6 = (bf16[128,16,128]{2,0,1:T(8,128)(2,1)S(1)}, bf16[128,16,128]{2,0,1:T(8,128)(2,1)}, u32[]{:S(2)}) copy-start(bf16[128,16,128]{2,0,1:T(8,128)(2,1)} %copy-done.5) | copy-start | bytes 1572868
  322.5 12.7 %copy-start.15 = (bf16[128,4,128]{2,1,0:T(4,128)(2,1)S(1)}, bf16[128,4,128]{2,1,0:T(4,128)(2,1)}, u32[]{:S(2)}) copy-start(bf16[128,4,128]{2,1,0:T(4,128)(2,1)} %param.16) | copy-start | bytes 393220
  327.6 21.2 %all-to-all-start.3 = ((f32[1024,2,128]{2,1,0:T(2,128)}), f32[1024,2,128]{2,1,0:T(2,128)}, u32[]{:S(2)}, u32[]{:S(2)}) async-start(f32[1024,2,128]{2,1,0:T(2,128)} %copy.176), calls=%async_computation.3 | async-start | bytes 2097152 | tf_op jit(solution)/shard_map/all_to_all | solution.py:203
  333.2 3.6 copy-start.11
  348.8 56.9 %all-to-all-start.4 = ((f32[8,128,2]{1,2,0:T(2,128)}), f32[8,128,2]{1,2,0:T(2,128)S(1)}, u32[]{:S(2)}, u32[]{:S(2)}) async-start(f32[8,128,2]{1,2,0:T(2,128)} %bitcast.65), calls=%async_computation.4 | async-start | bytes 16384 | tf_op jit(solution)/shard_map/all_to_all | solution.py:205
  354.1 0.8 copy-start.1
  361.4 0.8 copy-start.1
  368.8 0.8 copy-start.1
  376.1 0.8 copy-start.1
  383.4 0.8 copy-start.1
  390.7 0.8 copy-start.1
  398.1 0.8 copy-start.1
Sparse Core Ops, SparseCore 0:
  55.2 49.3 all-gather.3
  157.0 84.8 all-gather.5
where the time goes:
time: 417 us; the launch traced here: 415 us
  waiting for transfers between devices  147 us (35%)
  matrix products  115 us (28%)
  other arithmetic  54.8 us (13%)
  local copies, waits for them, and re-layouts  53.7 us (13%)
  starting transfers between devices  28.6 us (7%)
  between operations  13.9 us (3%)
    all_gather x1, waiting for transfers between devices, body(): lax.all_gather(block_map, 'key', axis=0, tiled=True)  44.1 us
    ppermute x3, waiting for transfers between devices, shifted(): lax.ppermute(value, axis, [(source, source + steps) for source in range(f...  42.5 us
    another operation x3, other arithmetic, block_terms(): lax.linalg.triangular_solve(system, right, left_side=True, lower=True, un...  39.4 us
    all_to_all x1, waiting for transfers between devices, body(): lax.all_to_all(key_slots, 'key', split_axis=1, concat_axis=0, tiled=True)  36.5 us
    dot_general x14, matrix products, attend(): jnp.einsum('...ij,...je->...ie', rounded, values, preferred_element_type=...  34.2 us
    dot_general x6, matrix products, one_block(): jnp.einsum('ie,je->ij', queries_flat, piece[:, :width], precision=highest)  22.7 us
    while x86, local copies, waits for them, and re-layouts  21.6 us
    dot_general x7, matrix products, replay_step(): moving = jnp.einsum('hie,hef->hif', moving, source_map, precision=highest)  14.3 us
  transfers between devices with their start and end apart: 10, of which 8 were waited for; matrix products, arithmetic and copies ran while one was open for 33% of the time, Pallas kernels for 0%

commit v1 on v0

--- a/solution.py
+++ b/solution.py
@@ -5,6 +5,18 @@
 from jax.sharding import PartitionSpec as P
 
 highest = lax.Precision.HIGHEST
+
+
+def collect(value, axis, dim):
+    ways, here, lap = (lax.axis_size(axis), lax.axis_index(axis), value.shape[dim])
+    shape = [n * ways if d == dim else n for d, n in enumerate(value.shape)]
+    full = lax.dynamic_update_slice_in_dim(
+        jnp.zeros(shape, value.dtype), value, here * lap, axis=dim
+    )
+    for far in range(1, ways):
+        value = lax.ppermute(value, axis, [(d, (d + 1) % ways) for d in range(ways)])
+        full = lax.dynamic_update_slice_in_dim(full, value, (here - far) % ways * lap, axis=dim)
+    return full
 
 
 def carried_in(value, axis, join, neutral, backward):
@@ -134,7 +146,7 @@
     packed = jnp.concatenate([key_end, value_head_rows.astype(jnp.float32)], axis=2)
     gathered_pack, gathered_maps = (
         lax.all_gather(packed, "key", axis=1, tiled=True),
-        lax.all_gather(block_map, "key", axis=0, tiled=True),
+        collect(block_map, "key", 0),
     )
     gathered_maps = gathered_maps.reshape(key_count, kv_heads, width, width)
 

time: 417 us -> 469 us (1.12)
  waiting for transfers between devices: 147 us -> 171 us
  starting transfers between devices: 28.6 us -> 46.8 us
  local copies, waits for them, and re-layouts: 53.7 us -> 59.2 us
    ppermute x0 -> x7, waiting for transfers between devices: none -> 57.1 us  [collect(): lax.ppermute(value, axis, [(d, (d + 1) % ways) for d in range(ways)])]
    all_to_all x1, waiting for transfers between devices: 36.5 us -> 15.3 us  [body(): lax.all_to_all(key_slots, 'key', split_axis=1, concat_axis=0, tiled=True)]
    ppermute x0 -> x7, starting transfers between devices: none -> 14 us  [collect(): lax.ppermute(value, axis, [(d, (d + 1) % ways) for d in range(ways)])]
    all_to_all x1, waiting for transfers between devices: 11 us -> 0.01 us  [body(): lax.all_to_all(far_sums, 'key', split_axis=0, concat_axis=1, tiled=True)]
    while x86, local copies, waits for them, and re-layouts: 21.6 us -> 15.8 us
    dynamic_update_slice x0 -> x8, local copies, waits for them, and re-layouts: none -> 5.78 us  [the longest x7 5.06 us: collect(): lax.dynamic_update_slice_in_dim(full, value, (here - far) % ways * lap, a...]
  transfers between devices with their start and end apart: 10 -> 17, of which waited for: 8 -> 13; matrix products, arithmetic and copies ran while one was open for 33% -> 33% of each run, Pallas kernels for 0% -> 0%
where the time goes in v1:
time: 469 us; the launch traced here: 466 us
  waiting for transfers between devices  171 us (36%)
  matrix products  116 us (25%)
  local copies, waits for them, and re-layouts  59.2 us (13%)
  other arithmetic  57.2 us (12%)
  starting transfers between devices  46.8 us (10%)
  between operations  14 us (3%)
    ppermute x7, waiting for transfers between devices, collect(): lax.ppermute(value, axis, [(d, (d + 1) % ways) for d in range(ways)])  57.1 us
    all_gather x1, waiting for transfers between devices, carried_in(): pieces = lax.all_gather(value, axis)  44.4 us
    ppermute x3, waiting for transfers between devices, shifted(): lax.ppermute(value, axis, [(source, source + steps) for source in range(f...  42.5 us
    another operation x3, other arithmetic, block_terms(): lax.linalg.triangular_solve(system, right, left_side=True, lower=True, un...  39.4 us
    dot_general x14, matrix products, attend(): jnp.einsum('...ij,...je->...ie', rounded, values, preferred_element_type=...  33.9 us
    dot_general x6, matrix products, one_block(): jnp.einsum('ie,je->ij', queries_flat, piece[:, :width], precision=highest)  22.7 us
    while x86, local copies, waits for them, and re-layouts  15.8 us
    all_to_all x1, waiting for transfers between devices, body(): lax.all_to_all(key_slots, 'key', split_axis=1, concat_axis=0, tiled=True)  15.3 us
  transfers between devices with their start and end apart: 17, of which 13 were waited for; matrix products, arithmetic and copies ran while one was open for 33% of the time, Pallas kernels for 0%

profile of v1, /device:TPU:6, one launch (start us, length us, event | category | flops | bytes accessed | tf_op | source)
XLA Modules:
  0.0 466.5 jit_solution(3632365724478160566)
XLA Ops:
  11.3 39.3 %custom-call.3 = f32[4,1,128,128]{2,3,1,0:T(8,128)S(1)} custom-call(f32[4,1,128,128]{3,2,1,0:T(8,128)S(1)} %fusion.41), custom_call_target="InvertDiagBlocksLowerTriangular" | custom-call | tf_op jit(solution)/shard_map/triangular_solve | solution.py:61
  58.4 44.4 %all-gather.6.cloned.1.call-done = f32[32,128,128]{2,1,0:T(8,128)} async-done(((f32[4,128,128]{2,1,0:T(8,128)}), f32[32,128,128]{2,1,0:T(8,128)}) %all-gather.6.cloned.1.call-update) | async-done | bytes 2097168 | tf_op jit(solution)/shard_map/all_gather | solution.py:24
  102.8 3.1 rev.3
  105.9 9.8 %while.97 = (s32[]{:T(128)}, f32[4,128,128]{2,1,0:T(8,128)S(1)}, s32[]{:T(128)}, f32[8,4,128,128]{3,2,1,0:T(8,128)}, s32[]{:T(128)}) while((s32[]{:T(128)}, f32[4,128,128]{2,1,0:T(8,128)S(1)}, s32[]{:T(128)}, f32[8,4,128,128]{3,2,1,0:T(8,128)}, s32[]{:T(128)}) %tuple.182), condition=%wide.region_10.11_spmd, body=%wide.region_9.10_spmd.sunk | while | flops 100728832 | bytes 1573447 | solution.py:34
  115.8 2.0 fusion.84
  117.8 4.9 %all-to-all-start.1 = ((f32[128,8,2,128]{3,0,2,1:T(8,128)}), f32[128,8,2,128]{3,0,2,1:T(8,128)S(1)}, u32[]{:S(2)}, u32[]{:S(2)}) async-start(f32[128,8,2,128]{3,0,2,1:T(8,128)} %bitcast.229), calls=%async_computation.1 | async-start | bytes 2097152 | tf_op jit(solution)/shard_map/all_to_all | solution.py:190
  122.8 11.4 %while.96 = (s32[]{:T(128)}, f32[4,128,128]{1,2,0:T(8,128)S(1)}, s32[]{:T(128)}, f32[8,4,128,128]{3,2,1,0:T(8,128)}, s32[]{:T(128)}) while((s32[]{:T(128)}, f32[4,128,128]{1,2,0:T(8,128)S(1)}, s32[]{:T(128)}, f32[8,4,128,128]{3,2,1,0:T(8,128)}, s32[]{:T(128)}) %tuple.165), condition=%wide.region_8.9_spmd, body=%wide.region_7.8_spmd.sunk | while | flops 100728832 | bytes 1573447 | solution.py:34
  136.5 10.5 %all-to-all-done.1 = f32[128,8,2,128]{3,0,2,1:T(8,128)S(1)} async-done(((f32[128,8,2,128]{3,0,2,1:T(8,128)}), f32[128,8,2,128]{3,0,2,1:T(8,128)S(1)}, u32[]{:S(2)}, u32[]{:S(2)}) %all-to-all-start.1) | async-done | bytes 1048608 | tf_op jit(solution)/shard_map/all_to_all | solution.py:190
  147.0 2.1 broadcast_in_dim.117
  149.1 4.9 %all-to-all-start = ((f32[128,8,256]{0,2,1:T(8,128)}), f32[128,8,256]{0,2,1:T(8,128)}, u32[]{:S(2)}, u32[]{:S(2)}) async-start(f32[128,8,256]{0,2,1:T(8,128)} %bitcast.228), calls=%async_computation | async-start | bytes 2097152 | tf_op jit(solution)/shard_map/all_to_all | solution.py:191
  159.1 2.8 fusion.54
  161.9 2.0 select_reduce_fusion.1
  163.9 20.5 %collective-permute-done.1 = f32[4,128,128]{2,1,0:T(8,128)} collective-permute-done((f32[4,128,128]{2,1,0:T(8,128)S(1)}, f32[4,128,128]{2,1,0:T(8,128)}, u32[]{:S(2)}, u32[]{:S(2)}) %collective-permute-start.1) | collective-permute-done | bytes 262176 | tf_op jit(solution)/shard_map/ppermute | solution.py:17
  184.3 3.5 collective-permute-start.2
  188.9 15.3 %all-to-all-done = f32[128,8,256]{0,2,1:T(8,128)} async-done(((f32[128,8,256]{0,2,1:T(8,128)}), f32[128,8,256]{0,2,1:T(8,128)}, u32[]{:S(2)}, u32[]{:S(2)}) %all-to-all-start) | async-done | bytes 1048608 | tf_op jit(solution)/shard_map/all_to_all | solution.py:191
  207.2 116.6 %while.99 = (s32[]{:T(128)}, f32[1024,256]{0,1:T(8,128)S(1)}, f32[2048]{0:T(1024)S(1)}, f32[2048]{0:T(1024)S(1)}, f32[2048,128]{1,0:T(8,128)}, /*index=5*/f32[12...) while((s32[]{:T(128)}, f32[1024,256]{0,1:T(8,128)S(1)}, ...), condition=%wide.region_16.17_spmd, body=%wide.region_11.16_spmd.sunk | while | flops 2094796800 | bytes 44106204 | solution.py:210
  207.2 2.1 collective-permute-start
  209.3 14.2 %collective-permute-done = f32[1024,256]{0,1:T(8,128)S(1)} collective-permute-done((f32[1024,256]{0,1:T(8,128)S(1)}, f32[1024,256]{0,1:T(8,128)S(1)}, u32[]{:S(2)}, u32[]{:S(2)}) %collective-permute-start) | collective-permute-done | bytes 1048608 | tf_op jit(solution)/shard_map/while/body/eval_jaxpr/ppermute | solution.py:40
  223.5 22.0 %while.100 = (s32[]{:T(128)}, f32[2048]{0:T(1024)S(1)}, f32[2048]{0:T(1024)S(1)}, f32[2048,128]{1,0:T(8,128)}, pred[]{:T(512)}, /*index=5*/f32[1024,256]{0,1:T(8...) while((s32[]{:T(128)}, f32[2048]{0:T(1024)S(1)}, ...), condition=%wide.region_15.15_spmd, body=%wide.region_12.14_spmd.sunk | while | flops 1893208064 | bytes 35651772 | solution.py:109
  223.7 3.8 fusion.150
  229.7 4.8 %convolution_add_fusion.6 = f32[2048,128]{1,0:T(8,128)} fusion(f32[512,2048]{1,0:T(8,128)} %copy-done, f32[2048]{0:T(1024)S(1)} %max.48, pred[]{:T(512)} %get-tuple-element.1047, f32[2048,128]{1,0:T(8,128)} %get-tuple-element.1035, f32[2048]{0:T(1024)S(1)} %get-tuple-element.1020, bf16[512,128]{1,0:T(8,128)(2,1)S(1)} %copy.289), kind=kOutput, calls=%fused_computation.33.clone.1 | convolution fusion | flops 274202624 | bytes 6438913 | tf_op jit(solution)/shard_map/while/body/eval_jaxpr/while/body/eval_jaxpr/...ij,...je->...ie/dot_general | solution.py:90
  234.7 3.8 fusion.150
  240.6 4.8 %convolution_add_fusion.6 = f32[2048,128]{1,0:T(8,128)} fusion(f32[512,2048]{1,0:T(8,128)} %copy-done, f32[2048]{0:T(1024)S(1)} %max.48, pred[]{:T(512)} %get-tuple-element.1047, f32[2048,128]{1,0:T(8,128)} %get-tuple-element.1035, f32[2048]{0:T(1024)S(1)} %get-tuple-element.1020, bf16[512,128]{1,0:T(8,128)(2,1)S(1)} %copy.289), kind=kOutput, calls=%fused_computation.33.clone.1 | convolution fusion | flops 274202624 | bytes 6438913 | tf_op jit(solution)/shard_map/while/body/eval_jaxpr/while/body/eval_jaxpr/...ij,...je->...ie/dot_general | solution.py:90
  248.2 14.2 %collective-permute-done = f32[1024,256]{0,1:T(8,128)S(1)} collective-permute-done((f32[1024,256]{0,1:T(8,128)S(1)}, f32[1024,256]{0,1:T(8,128)S(1)}, u32[]{:S(2)}, u32[]{:S(2)}) %collective-permute-start) | collective-permute-done | bytes 1048608 | tf_op jit(solution)/shard_map/while/body/eval_jaxpr/ppermute | solution.py:40
  262.3 21.9 %while.100 = (s32[]{:T(128)}, f32[2048]{0:T(1024)S(1)}, f32[2048]{0:T(1024)S(1)}, f32[2048,128]{1,0:T(8,128)}, pred[]{:T(512)}, /*index=5*/f32[1024,256]{0,1:T(8...) while((s32[]{:T(128)}, f32[2048]{0:T(1024)S(1)}, ...), condition=%wide.region_15.15_spmd, body=%wide.region_12.14_spmd.sunk | while | flops 1893208064 | bytes 35651772 | solution.py:109
  262.5 3.8 fusion.150
  268.5 4.8 %convolution_add_fusion.6 = f32[2048,128]{1,0:T(8,128)} fusion(f32[512,2048]{1,0:T(8,128)} %copy-done, f32[2048]{0:T(1024)S(1)} %max.48, pred[]{:T(512)} %get-tuple-element.1047, f32[2048,128]{1,0:T(8,128)} %get-tuple-element.1035, f32[2048]{0:T(1024)S(1)} %get-tuple-element.1020, bf16[512,128]{1,0:T(8,128)(2,1)S(1)} %copy.289), kind=kOutput, calls=%fused_computation.33.clone.1 | convolution fusion | flops 274202624 | bytes 6438913 | tf_op jit(solution)/shard_map/while/body/eval_jaxpr/while/body/eval_jaxpr/...ij,...je->...ie/dot_general | solution.py:90
  273.5 3.8 fusion.150
  279.5 4.8 %convolution_add_fusion.6 = f32[2048,128]{1,0:T(8,128)} fusion(f32[512,2048]{1,0:T(8,128)} %copy-done, f32[2048]{0:T(1024)S(1)} %max.48, pred[]{:T(512)} %get-tuple-element.1047, f32[2048,128]{1,0:T(8,128)} %get-tuple-element.1035, f32[2048]{0:T(1024)S(1)} %get-tuple-element.1020, bf16[512,128]{1,0:T(8,128)(2,1)S(1)} %copy.289), kind=kOutput, calls=%fused_computation.33.clone.1 | convolution fusion | flops 274202624 | bytes 6438913 | tf_op jit(solution)/shard_map/while/body/eval_jaxpr/while/body/eval_jaxpr/...ij,...je->...ie/dot_general | solution.py:90
  286.9 14.2 %collective-permute-done = f32[1024,256]{0,1:T(8,128)S(1)} collective-permute-done((f32[1024,256]{0,1:T(8,128)S(1)}, f32[1024,256]{0,1:T(8,128)S(1)}, u32[]{:S(2)}, u32[]{:S(2)}) %collective-permute-start) | collective-permute-done | bytes 1048608 | tf_op jit(solution)/shard_map/while/body/eval_jaxpr/ppermute | solution.py:40
  301.1 21.9 %while.100 = (s32[]{:T(128)}, f32[2048]{0:T(1024)S(1)}, f32[2048]{0:T(1024)S(1)}, f32[2048,128]{1,0:T(8,128)}, pred[]{:T(512)}, /*index=5*/f32[1024,256]{0,1:T(8...) while((s32[]{:T(128)}, f32[2048]{0:T(1024)S(1)}, ...), condition=%wide.region_15.15_spmd, body=%wide.region_12.14_spmd.sunk | while | flops 1893208064 | bytes 35651772 | solution.py:109
  301.3 3.8 fusion.150
  307.3 4.8 %convolution_add_fusion.6 = f32[2048,128]{1,0:T(8,128)} fusion(f32[512,2048]{1,0:T(8,128)} %copy-done, f32[2048]{0:T(1024)S(1)} %max.48, pred[]{:T(512)} %get-tuple-element.1047, f32[2048,128]{1,0:T(8,128)} %get-tuple-element.1035, f32[2048]{0:T(1024)S(1)} %get-tuple-element.1020, bf16[512,128]{1,0:T(8,128)(2,1)S(1)} %copy.289), kind=kOutput, calls=%fused_computation.33.clone.1 | convolution fusion | flops 274202624 | bytes 6438913 | tf_op jit(solution)/shard_map/while/body/eval_jaxpr/while/body/eval_jaxpr/...ij,...je->...ie/dot_general | solution.py:90
  312.3 3.8 fusion.150
  318.3 4.8 %convolution_add_fusion.6 = f32[2048,128]{1,0:T(8,128)} fusion(f32[512,2048]{1,0:T(8,128)} %copy-done, f32[2048]{0:T(1024)S(1)} %max.48, pred[]{:T(512)} %get-tuple-element.1047, f32[2048,128]{1,0:T(8,128)} %get-tuple-element.1035, f32[2048]{0:T(1024)S(1)} %get-tuple-element.1020, bf16[512,128]{1,0:T(8,128)(2,1)S(1)} %copy.289), kind=kOutput, calls=%fused_computation.33.clone.1 | convolution fusion | flops 274202624 | bytes 6438913 | tf_op jit(solution)/shard_map/while/body/eval_jaxpr/while/body/eval_jaxpr/...ij,...je->...ie/dot_general | solution.py:90
  324.4 3.5 all-to-all-start.2
  328.1 3.2 copy.211
  332.9 5.6 %all-to-all-start.3 = ((f32[1024,2,128]{2,1,0:T(2,128)}), f32[1024,2,128]{2,1,0:T(2,128)}, u32[]{:S(2)}, u32[]{:S(2)}) async-start(f32[1024,2,128]{2,1,0:T(2,128)} %copy.211), calls=%async_computation.3 | async-start | bytes 2097152 | tf_op jit(solution)/shard_map/all_to_all | solution.py:215
  343.4 12.5 %collective-permute-done.3 = f32[4,128,128]{2,1,0:T(8,128)} collective-permute-done((f32[4,128,128]{2,1,0:T(8,128)}, f32[4,128,128]{2,1,0:T(8,128)}, u32[]{:S(2)}, u32[]{:S(2)}) %collective-permute-start.3) | collective-permute-done | bytes 262176 | tf_op jit(solution)/shard_map/ppermute | solution.py:17
  355.9 3.4 collective-permute-start.4
  359.6 6.6 %collective-permute-done.4 = f32[4,128,128]{2,1,0:T(8,128)S(1)} collective-permute-done((f32[4,128,128]{2,1,0:T(8,128)}, f32[4,128,128]{2,1,0:T(8,128)S(1)}, u32[]{:S(2)}, u32[]{:S(2)}) %collective-permute-start.4) | collective-permute-done | bytes 262176 | tf_op jit(solution)/shard_map/ppermute | solution.py:17
  366.2 3.3 collective-permute-start.5
  371.0 7.2 %collective-permute-done.5 = f32[4,128,128]{2,1,0:T(8,128)S(1)} collective-permute-done((f32[4,128,128]{2,1,0:T(8,128)S(1)}, f32[4,128,128]{2,1,0:T(8,128)S(1)}, u32[]{:S(2)}, u32[]{:S(2)}) %collective-permute-start.5) | collective-permute-done | bytes 262176 | tf_op jit(solution)/shard_map/ppermute | solution.py:17
  383.2 3.7 collective-permute-done.6
  389.3 6.7 %collective-permute-done.7 = f32[4,128,128]{2,1,0:T(8,128)S(1)} collective-permute-done((f32[4,128,128]{2,1,0:T(8,128)S(1)}, f32[4,128,128]{2,1,0:T(8,128)S(1)}, u32[]{:S(2)}, u32[]{:S(2)}) %collective-permute-start.7) | collective-permute-done | bytes 262176 | tf_op jit(solution)/shard_map/ppermute | solution.py:17
  397.5 7.9 %all-to-all-start.4 = ((f32[8,128,2]{1,2,0:T(2,128)}), f32[8,128,2]{1,2,0:T(2,128)S(1)}, u32[]{:S(2)}, u32[]{:S(2)}) async-start(f32[8,128,2]{1,2,0:T(2,128)} %bitcast.66), calls=%async_computation.4 | async-start | bytes 16384 | tf_op jit(solution)/shard_map/all_to_all | solution.py:217
  405.4 50.5 %while.95 = (s32[]{:T(128)}, f32[4,512,128]{1,2,0:T(8,128)S(1)}, f32[4,512]{1,0:T(4,128)S(1)}, f32[4,512]{1,0:T(4,128)S(1)}, f32[4,512,128]{2,1,0:T(8,128)S(1)},...) while((s32[]{:T(128)}, f32[4,512,128]{1,2,0:T(8,128)S(1)}, ...), condition=%wide.region_6.7_spmd, body=%wide.region_3.6_spmd.sunk | while | flops 875302912 | bytes 15991019 | solution.py:168
  417.9 1.9 convolution_bitcast_fusion.5
  (325 shorter events, 133.8 us)
Async XLA Ops:
  6.5 44.3 %copy-start.8 = (bf16[128,4,128]{2,1,0:T(4,128)(2,1)S(1)}, bf16[128,4,128]{2,1,0:T(4,128)(2,1)}, u32[]{:S(2)}) copy-start(bf16[128,4,128]{2,1,0:T(4,128)(2,1)} %param.18) | copy-start | bytes 393220
  6.5 44.1 %copy-start.13 = (bf16[128,4,128]{2,1,0:T(4,128)(2,1)S(1)}, bf16[128,4,128]{2,1,0:T(4,128)(2,1)}, u32[]{:S(2)}) copy-start(bf16[128,4,128]{2,1,0:T(4,128)(2,1)} %param.16) | copy-start | bytes 393220
  6.5 96.2 %all-gather.6.cloned.1.call-start = ((), (), s32[]{:S(2)}) async-start(), calls=%async_computation.6 | async-start | bytes 2359296 | tf_op jit(solution)/shard_map/all_gather | solution.py:24
  50.8 2.5 copy-start.12
  51.2 2.3 copy-start.17
  51.8 4.7 %copy-start.7 = (f32[4,128,256]{2,1,0:T(8,128)}, f32[4,128,256]{2,1,0:T(8,128)S(1)}, u32[]{:S(2)}) copy-start(f32[4,128,256]{2,1,0:T(8,128)S(1)} %fusion.49) | copy-start | bytes 1572868
  53.7 2.2 copy-start.9
  58.4 57.4 %copy-start.3 = (f32[4,4,128,128]{3,2,1,0:T(8,128)}, f32[4,4,128,128]{3,2,1,0:T(8,128)S(1)}, u32[]{:S(2)}) copy-start(f32[4,4,128,128]{3,2,1,0:T(8,128)S(1)} %convolution_subtract_fusion.1) | copy-start | bytes 3145732
  117.8 29.2 %all-to-all-start.1 = ((f32[128,8,2,128]{3,0,2,1:T(8,128)}), f32[128,8,2,128]{3,0,2,1:T(8,128)S(1)}, u32[]{:S(2)}, u32[]{:S(2)}) async-start(f32[128,8,2,128]{3,0,2,1:T(8,128)} %bitcast.229), calls=%async_computation.1 | async-start | bytes 2097152 | tf_op jit(solution)/shard_map/all_to_all | solution.py:190
  122.7 11.4 %copy-start.11 = (f32[4,128,128]{1,2,0:T(8,128)S(1)}, f32[4,128,128]{1,2,0:T(8,128)}, u32[]{:S(2)}) copy-start(f32[4,128,128]{1,2,0:T(8,128)} %convolution_subtract_fusion.2) | copy-start | bytes 786436
  136.5 17.6 %copy-start.5 = (f32[4,128,128]{2,1,0:T(8,128)S(1)}, f32[4,128,128]{2,1,0:T(8,128)}, u32[]{:S(2)}) copy-start(f32[4,128,128]{2,1,0:T(8,128)} %convolution_subtract_fusion.3) | copy-start | bytes 786436
  149.1 55.1 %all-to-all-start = ((f32[128,8,256]{0,2,1:T(8,128)}), f32[128,8,256]{0,2,1:T(8,128)}, u32[]{:S(2)}, u32[]{:S(2)}) async-start(f32[128,8,256]{0,2,1:T(8,128)} %bitcast.228), calls=%async_computation | async-start | bytes 2097152 | tf_op jit(solution)/shard_map/all_to_all | solution.py:191
  154.1 7.8 %copy-start.14 = (bf16[128,4,128]{2,1,0:T(4,128)(2,1)S(1)}, bf16[128,4,128]{2,1,0:T(4,128)(2,1)}, u32[]{:S(2)}) copy-start(bf16[128,4,128]{2,1,0:T(4,128)(2,1)} %param.16) | copy-start | bytes 393220
  154.1 251.4 %all-gather.4.cloned.1.call-start = ((), (), s32[]{:S(2)}) async-start(), calls=%async_computation.5 | async-start | bytes 4718592 | tf_op jit(solution)/shard_map/all_gather | solution.py:148
  154.1 30.3 %collective-permute-start.1 = (f32[4,128,128]{2,1,0:T(8,128)S(1)}, f32[4,128,128]{2,1,0:T(8,128)}, u32[]{:S(2)}, u32[]{:S(2)}) collective-permute-start(f32[4,128,128]{2,1,0:T(8,128)S(1)} %copy-done.5), channel_id=1, source_target_pairs={{0,1},{1,2},{2,3},{3,4},{4,5},{5,6},{6,7},{7,0},{8,9},{9,10},{10,1... | collective-permute-start | bytes 786440 | tf_op jit(solution)/shard_map/ppermute | solution.py:17
  159.1 4.8 %copy-start.15 = (pred[128,128]{1,0:T(8,128)(4,1)}, pred[128,128]{1,0:T(8,128)(4,1)S(1)}, u32[]{:S(2)}) copy-start(pred[128,128]{1,0:T(8,128)(4,1)S(1)} %copy.183) | copy-start | bytes 49156
  184.3 154.8 %collective-permute-start.2 = (f32[4,128,128]{2,1,0:T(8,128)}, f32[4,128,128]{2,1,0:T(8,128)}, u32[]{:S(2)}, u32[]{:S(2)}) collective-permute-start(f32[4,128,128]{2,1,0:T(8,128)} %collective-permute-done.1), channel_id=1, source_target_pairs={{0,1},{1,2},{2,3},{3,4},{4,5},{5,6},{6,7},{7,0},{8,9},{9,10},{10,1... | collective-permute-start | bytes 786440 | tf_op jit(solution)/shard_map/ppermute | solution.py:17
  207.2 120.7 %copy-start.18 = (f32[4,4,128]{2,1,0:T(4,128)S(1)}, f32[4,4,128]{2,1,0:T(4,128)}, u32[]{:S(2)}) copy-start(f32[4,4,128]{2,1,0:T(4,128)} %get-tuple-element.785) | copy-start | bytes 24580
  207.2 120.7 %copy-start.6 = (f32[4,128,128]{2,1,0:T(8,128)S(1)}, f32[4,128,128]{2,1,0:T(8,128)}, u32[]{:S(2)}) copy-start(f32[4,128,128]{2,1,0:T(8,128)} %convolution_subtract_fusion.3) | copy-start | bytes 786436
  207.2 16.2 %collective-permute-start = (f32[1024,256]{0,1:T(8,128)S(1)}, f32[1024,256]{0,1:T(8,128)S(1)}, u32[]{:S(2)}, u32[]{:S(2)}) collective-permute-start(f32[1024,256]{0,1:T(8,128)S(1)} %get-tuple-element.1099), channel_id=1, source_target_pairs={{0,8},{8,16},{16,24},{1,9},{9,17},{17,25},{2,10},{10,18},{18,26},{... | collective-permute-start | bytes 3145736 | tf_op jit(solution)/shard_map/while/body/eval_jaxpr/ppermute | solution.py:40
  227.5 2.0 copy-start
  238.5 2.0 copy-start
  246.2 16.1 %collective-permute-start = (f32[1024,256]{0,1:T(8,128)S(1)}, f32[1024,256]{0,1:T(8,128)S(1)}, u32[]{:S(2)}, u32[]{:S(2)}) collective-permute-start(f32[1024,256]{0,1:T(8,128)S(1)} %get-tuple-element.1099), channel_id=1, source_target_pairs={{0,8},{8,16},{16,24},{1,9},{9,17},{17,25},{2,10},{10,18},{18,26},{... | collective-permute-start | bytes 3145736 | tf_op jit(solution)/shard_map/while/body/eval_jaxpr/ppermute | solution.py:40
  266.3 2.0 copy-start
  277.3 2.0 copy-start
  285.0 16.1 %collective-permute-start = (f32[1024,256]{0,1:T(8,128)S(1)}, f32[1024,256]{0,1:T(8,128)S(1)}, u32[]{:S(2)}, u32[]{:S(2)}) collective-permute-start(f32[1024,256]{0,1:T(8,128)S(1)} %get-tuple-element.1099), channel_id=1, source_target_pairs={{0,8},{8,16},{16,24},{1,9},{9,17},{17,25},{2,10},{10,18},{18,26},{... | collective-permute-start | bytes 3145736 | tf_op jit(solution)/shard_map/while/body/eval_jaxpr/ppermute | solution.py:40
  305.1 2.0 copy-start
  316.1 2.0 copy-start
  324.4 8.5 %all-to-all-start.2 = ((f32[8,128,2]{1,2,0:T(2,128)}), f32[8,128,2]{1,2,0:T(2,128)S(1)}, u32[]{:S(2)}, u32[]{:S(2)}) async-start(f32[8,128,2]{1,2,0:T(2,128)} %bitcast.54), calls=%async_computation.2 | async-start | bytes 16384 | tf_op jit(solution)/shard_map/all_to_all | solution.py:216
  328.1 10.4 %copy-start.2 = (f32[4,4,128,128]{3,2,1,0:T(8,128)S(1)}, f32[4,4,128,128]{3,2,1,0:T(8,128)}, u32[]{:S(2)}) copy-start(f32[4,4,128,128]{3,2,1,0:T(8,128)} %get-tuple-element.786) | copy-start | bytes 3145732
  328.1 10.4 %copy-start.16 = (pred[128,128]{1,0:T(8,128)(4,1)S(1)}, pred[128,128]{1,0:T(8,128)(4,1)}, u32[]{:S(2)}) copy-start(pred[128,128]{1,0:T(8,128)(4,1)} %copy-done.15) | copy-start | bytes 49156
  332.9 64.6 %all-to-all-start.3 = ((f32[1024,2,128]{2,1,0:T(2,128)}), f32[1024,2,128]{2,1,0:T(2,128)}, u32[]{:S(2)}, u32[]{:S(2)}) async-start(f32[1024,2,128]{2,1,0:T(2,128)} %copy.211), calls=%async_computation.3 | async-start | bytes 2097152 | tf_op jit(solution)/shard_map/all_to_all | solution.py:215
  338.5 4.5 copy-start.4
  339.1 16.7 %collective-permute-start.3 = (f32[4,128,128]{2,1,0:T(8,128)}, f32[4,128,128]{2,1,0:T(8,128)}, u32[]{:S(2)}, u32[]{:S(2)}) collective-permute-start(f32[4,128,128]{2,1,0:T(8,128)} %collective-permute-done.2), channel_id=1, source_target_pairs={{0,1},{1,2},{2,3},{3,4},{4,5},{5,6},{6,7},{7,0},{8,9},{9,10},{10,1... | collective-permute-start | bytes 786440 | tf_op jit(solution)/shard_map/ppermute | solution.py:17
  343.0 26.5 %copy-start.10 = (bf16[128,4,128]{0,2,1:T(8,128)(2,1)S(1)}, bf16[128,4,128]{0,2,1:T(8,128)(2,1)}, u32[]{:S(2)}) copy-start(bf16[128,4,128]{0,2,1:T(8,128)(2,1)} %copy-done.9) | copy-start | bytes 393220
  355.9 10.4 %collective-permute-start.4 = (f32[4,128,128]{2,1,0:T(8,128)}, f32[4,128,128]{2,1,0:T(8,128)S(1)}, u32[]{:S(2)}, u32[]{:S(2)}) collective-permute-start(f32[4,128,128]{2,1,0:T(8,128)} %collective-permute-done.3), channel_id=1, source_target_pairs={{0,1},{1,2},{2,3},{3,4},{4,5},{5,6},{6,7},{7,0},{8,9},{9,10},{10,1... | collective-permute-start | bytes 786440 | tf_op jit(solution)/shard_map/ppermute | solution.py:17
  366.2 11.9 %collective-permute-start.5 = (f32[4,128,128]{2,1,0:T(8,128)S(1)}, f32[4,128,128]{2,1,0:T(8,128)S(1)}, u32[]{:S(2)}, u32[]{:S(2)}) collective-permute-start(f32[4,128,128]{2,1,0:T(8,128)S(1)} %collective-permute-done.4), channel_id=1, source_target_pairs={{0,1},{1,2},{2,3},{3,4},{4,5},{5,6},{6,7},{7,0},{8,9},{9,10},{10,1... | collective-permute-start | bytes 786440 | tf_op jit(solution)/shard_map/ppermute | solution.py:17
  378.1 8.8 %collective-permute-start.6 = (f32[4,128,128]{2,1,0:T(8,128)S(1)}, f32[4,128,128]{2,1,0:T(8,128)S(1)}, u32[]{:S(2)}, u32[]{:S(2)}) collective-permute-start(f32[4,128,128]{2,1,0:T(8,128)S(1)} %collective-permute-done.5), channel_id=1, source_target_pairs={{0,1},{1,2},{2,3},{3,4},{4,5},{5,6},{6,7},{7,0},{8,9},{9,10},{10,1... | collective-permute-start | bytes 786440 | tf_op jit(solution)/shard_map/ppermute | solution.py:17
  386.9 9.1 %collective-permute-start.7 = (f32[4,128,128]{2,1,0:T(8,128)S(1)}, f32[4,128,128]{2,1,0:T(8,128)S(1)}, u32[]{:S(2)}, u32[]{:S(2)}) collective-permute-start(f32[4,128,128]{2,1,0:T(8,128)S(1)} %collective-permute-done.6), channel_id=1, source_target_pairs={{0,1},{1,2},{2,3},{3,4},{4,5},{5,6},{6,7},{7,0},{8,9},{9,10},{10,1... | collective-permute-start | bytes 786440 | tf_op jit(solution)/shard_map/ppermute | solution.py:17
  397.5 59.9 %all-to-all-start.4 = ((f32[8,128,2]{1,2,0:T(2,128)}), f32[8,128,2]{1,2,0:T(2,128)S(1)}, u32[]{:S(2)}, u32[]{:S(2)}) async-start(f32[8,128,2]{1,2,0:T(2,128)} %bitcast.66), calls=%async_computation.4 | async-start | bytes 16384 | tf_op jit(solution)/shard_map/all_to_all | solution.py:217
  406.5 0.8 copy-start.1
  413.7 0.8 copy-start.1
  421.0 0.8 copy-start.1
  428.2 0.8 copy-start.1
  435.4 0.8 copy-start.1
  442.6 0.8 copy-start.1
  449.9 0.8 copy-start.1
Sparse Core Ops, SparseCore 0:
  53.4 49.3 all-gather.5
  157.8 94.5 all-gather.3
